TPU v7x, 32 devices: a whole 2x2x4 slice. The times are simulated.
32 devices in a mesh: dp: 8 (over z, y), ctx: 4 (over x, core).
Axes of the slice: x: 2, y: 2, z: 4, core: 2. Of those that a mesh axis runs over, the one named last changes fastest.
Arguments:
- tokens: bfloat16 [8, 1024, 2048], P('dp', 'ctx'), may hold values from -6 to 6
- cotangent: bfloat16 [8, 1024, 2048], P('dp', 'ctx'), may hold values from -6 to 6
- domain_ids: int32 [8], P('dp'), may hold values from 0 to 31
- domain_counts: int32 [32], replicated, may hold values from 1024 to 4096
- domain_numer: int32 [32], replicated, may hold values from 1 to 8
- domain_denom: int32 [32], replicated, may hold values from 1 to 8
- attention_gain: bfloat16 [2048], replicated, may hold values from 0.5 to 1.5
- query_gain: bfloat16 [128], replicated, may hold values from 0.796875 to 1.796875
- key_gain: bfloat16 [128], replicated, may hold values from 0.796875 to 1.796875
- query_proj: bfloat16 [2048, 2048], P('dp', 'ctx'), may hold values from -0.125 to 0.125
- key_proj: bfloat16 [2048, 1024], P('dp', 'ctx'), may hold values from -0.125 to 0.125
- value_proj: bfloat16 [2048, 1024], P('dp', 'ctx'), may hold values from -0.125 to 0.125
- gating_proj: bfloat16 [2048, 2048], P('dp', 'ctx'), may hold values from -0.125 to 0.125
- output_proj: bfloat16 [2048, 2048], P('ctx', 'dp'), may hold values from -1 to 1
- swiglu_gain: bfloat16 [2048], replicated, may hold values from 0.5 to 1.5
- swiglu_gate: bfloat16 [2048, 6144], P('dp', 'ctx'), may hold values from -0.125 to 0.125
- swiglu_up: bfloat16 [2048, 6144], P('dp', 'ctx'), may hold values from -0.125 to 0.125
- swiglu_down: bfloat16 [6144, 2048], P('ctx', 'dp'), may hold values from -0.109375 to 0.109375
Outputs:
- layer_out: bfloat16 [8, 1024, 2048], P('dp', 'ctx')
- input_grad: bfloat16 [8, 1024, 2048], P('dp', 'ctx')
- attention_gain_grad: float32 [2048], replicated
- query_gain_grad: float32 [128], replicated
- key_gain_grad: float32 [128], replicated
- query_proj_grad: float32 [2048, 2048], P('dp', 'ctx')
- key_proj_grad: float32 [2048, 1024], P('dp', 'ctx')
- value_proj_grad: float32 [2048, 1024], P('dp', 'ctx')
- gating_proj_grad: float32 [2048, 2048], P('dp', 'ctx')
- output_proj_grad: float32 [2048, 2048], P('ctx', 'dp')
- swiglu_gain_grad: float32 [2048], replicated
- swiglu_gate_grad: float32 [2048, 6144], P('dp', 'ctx')
- swiglu_up_grad: float32 [2048, 6144], P('dp', 'ctx')
- swiglu_down_grad: float32 [6144, 2048], P('ctx', 'dp')
All inputs are finite; a program needn't handle non-finite values.
Results may differ from a plain program's by a relative error of at most 0.019.
Values may be sent and summed in bfloat16 or wider, within the bound.
A program may use at most 192 MiB of HBM per device.

v0:
```python
import jax
import jax.numpy as jnp
from jax import lax
from jax.sharding import PartitionSpec as P

LENGTH = 1024


EPSILON = 1e-06
ROPE_BASE = 1000000.0


def matmul_f32(left, right):
    return jnp.dot(left, right, preferred_element_type=jnp.float32)


def matmul_tn(left, right):
    return lax.dot_general(
        left, right, (((0,), (0,)), ((), ())), preferred_element_type=jnp.float32
    )


def matmul_nt(left, right):
    return lax.dot_general(
        left, right, (((1,), (1,)), ((), ())), preferred_element_type=jnp.float32
    )


def rope_tables(positions, head_width):
    halfway = head_width // 2
    inverse = 1.0 / ROPE_BASE ** (jnp.arange(halfway, dtype=jnp.float32) * (2.0 / head_width))
    angles = positions.astype(jnp.float32)[:, None] * inverse[None, :]
    return (jnp.cos(angles), jnp.sin(angles))


def rotate(tensor, cosine, sine):
    halfway = tensor.shape[-1] // 2
    first_half = tensor[..., :halfway]
    second_half = tensor[..., halfway:]
    return jnp.concatenate(
        [first_half * cosine - second_half * sine, second_half * cosine + first_half * sine], -1
    )


def unrotate(grads_in, cosine, sine):
    halfway = grads_in.shape[-1] // 2
    first_half = grads_in[..., :halfway]
    second_half = grads_in[..., halfway:]
    return jnp.concatenate(
        [first_half * cosine + second_half * sine, second_half * cosine - first_half * sine], -1
    )


def norm_back(grads_in, values_in, inverse, gain_vec):
    scaled = grads_in * gain_vec
    return inverse * scaled - values_in * (inverse * inverse * inverse) * jnp.mean(
        scaled * values_in, -1, keepdims=True
    )


def attention_weights(query_proj, key_proj, value_proj, gating_proj, output_proj):
    return (
        lax.all_gather(query_proj, "dp", axis=0, tiled=True),
        lax.all_gather(key_proj, "dp", axis=0, tiled=True),
        lax.all_gather(value_proj, "dp", axis=0, tiled=True),
        lax.all_gather(gating_proj, "dp", axis=0, tiled=True),
        lax.all_gather(output_proj, "dp", axis=1, tiled=True),
    )


def swiglu_weights(swiglu_gate, swiglu_up, swiglu_down):
    return (
        lax.all_gather(swiglu_gate, "dp", axis=0, tiled=True),
        lax.all_gather(swiglu_up, "dp", axis=0, tiled=True),
        lax.all_gather(swiglu_down, "dp", axis=1, tiled=True),
    )


def softmax_forward(seq_items, causal):
    queries, keys_seq, values_seq = seq_items
    scaling = queries.shape[-1] ** (-0.5)
    scores = (
        jnp.einsum("qgjd,kgd->gjqk", queries, keys_seq, preferred_element_type=jnp.float32)
        * scaling
    )
    scores = jnp.where(causal, scores, -1e30)
    highest = jnp.max(scores, -1, keepdims=True)
    exp_vals = jnp.exp(scores - highest)
    row_totals = jnp.sum(exp_vals, -1, keepdims=True)
    attn_probs = (exp_vals / row_totals).astype(jnp.bfloat16)
    attended = jnp.einsum(
        "gjqk,kgd->qgjd", attn_probs, values_seq, preferred_element_type=jnp.float32
    )
    return (attended, highest[..., 0] + jnp.log(row_totals[..., 0]))


def softmax_backward(seq_items, causal):
    queries, keys_seq, values_seq, log_total, upstream = seq_items
    scaling = queries.shape[-1] ** (-0.5)
    scores = (
        jnp.einsum("qgjd,kgd->gjqk", queries, keys_seq, preferred_element_type=jnp.float32)
        * scaling
    )
    scores = jnp.where(causal, scores, -1e30)
    attn_probs = jnp.exp(scores - log_total[..., None])
    dprobs = jnp.einsum("qgjd,kgd->gjqk", upstream, values_seq, preferred_element_type=jnp.float32)
    centre = jnp.sum(dprobs * attn_probs, -1, keepdims=True)
    dscores = (attn_probs * (dprobs - centre)).astype(jnp.bfloat16)
    dqueries = (
        jnp.einsum("gjqk,kgd->qgjd", dscores, keys_seq, preferred_element_type=jnp.float32)
        * scaling
    )
    key_grads = (
        jnp.einsum("gjqk,qgjd->kgd", dscores, queries, preferred_element_type=jnp.float32) * scaling
    )
    value_grads = jnp.einsum(
        "gjqk,qgjd->kgd",
        attn_probs.astype(jnp.bfloat16),
        upstream,
        preferred_element_type=jnp.float32,
    )
    key_rows = key_grads.shape[0]
    return (dqueries, key_grads.reshape(key_rows, -1), value_grads.reshape(key_rows, -1))


def per_device(
    tokens,
    cotangent,
    domain_ids,
    domain_counts,
    domain_numer,
    domain_denom,
    attention_gain,
    query_gain,
    key_gain,
    query_proj,
    key_proj,
    value_proj,
    gating_proj,
    output_proj,
    swiglu_gain,
    swiglu_gate,
    swiglu_up,
    swiglu_down,
):
    seq_count, local_len, model_width = tokens.shape
    full_len = local_len * lax.axis_size("ctx")
    local_rows = seq_count * local_len
    all_rows = seq_count * full_len
    head_dim = query_gain.shape[0]
    local_heads = query_proj.shape[1] // head_dim
    local_kv = key_proj.shape[1] // head_dim
    group_size = local_heads // local_kv
    positions = jnp.arange(full_len, dtype=jnp.int32)
    causal = positions[:, None] >= positions[None, :]
    cosine, sine = rope_tables(positions, head_dim)
    cos_rows = cosine[:, None, :]
    sin_rows = sine[:, None, :]
    inputs = tokens.reshape(local_rows, model_width).astype(jnp.float32)
    inverse_in = lax.rsqrt(jnp.mean(inputs * inputs, -1, keepdims=True) + EPSILON)
    gain_in = attention_gain.astype(jnp.float32)
    normed = (inputs * inverse_in * gain_in).astype(jnp.bfloat16)
    normed_all = lax.all_gather(
        normed.reshape(seq_count, local_len, model_width), "ctx", axis=1, tiled=True
    ).reshape(all_rows, model_width)
    attn_full = attention_weights(query_proj, key_proj, value_proj, gating_proj, output_proj)
    query_raw = matmul_f32(normed_all, attn_full[0]).reshape(
        seq_count, full_len, local_heads, head_dim
    )
    key_raw = matmul_f32(normed_all, attn_full[1]).reshape(seq_count, full_len, local_kv, head_dim)
    value_low = (
        matmul_f32(normed_all, attn_full[2])
        .astype(jnp.bfloat16)
        .reshape(seq_count, full_len, local_kv, head_dim)
    )
    gate_pre = matmul_f32(normed_all, attn_full[3])
    query_scale = query_gain.astype(jnp.float32)
    key_scale = key_gain.astype(jnp.float32)
    query_inv = lax.rsqrt(jnp.mean(query_raw * query_raw, -1, keepdims=True) + EPSILON)
    key_inv = lax.rsqrt(jnp.mean(key_raw * key_raw, -1, keepdims=True) + EPSILON)
    query_low = rotate(query_raw * query_inv * query_scale, cos_rows, sin_rows).astype(jnp.bfloat16)
    key_low = rotate(key_raw * key_inv * key_scale, cos_rows, sin_rows).astype(jnp.bfloat16)
    query_groups = query_low.reshape(seq_count, full_len, local_kv, group_size, head_dim)
    attended, log_total = lax.map(
        lambda seq_items: softmax_forward(seq_items, causal), (query_groups, key_low, value_low)
    )
    attended = attended.reshape(all_rows, local_heads * head_dim)
    gate_sig = jax.nn.sigmoid(gate_pre)
    mixed = (attended * gate_sig).astype(jnp.bfloat16)
    branch_part = matmul_f32(mixed, attn_full[4]).reshape(seq_count, full_len, model_width)
    branch = lax.psum_scatter(branch_part, "ctx", scatter_dimension=1, tiled=True).reshape(
        local_rows, model_width
    )
    hidden = inputs + branch
    inverse_mid = lax.rsqrt(jnp.mean(hidden * hidden, -1, keepdims=True) + EPSILON)
    gain_mid = swiglu_gain.astype(jnp.float32)
    normed_mid = (hidden * inverse_mid * gain_mid).astype(jnp.bfloat16)
    normed_mid_all = lax.all_gather(
        normed_mid.reshape(seq_count, local_len, model_width), "ctx", axis=1, tiled=True
    ).reshape(all_rows, model_width)
    swiglu_full = swiglu_weights(swiglu_gate, swiglu_up, swiglu_down)
    gate_ff = matmul_f32(normed_mid_all, swiglu_full[0])
    up_val = matmul_f32(normed_mid_all, swiglu_full[1])
    gate_sigma = jax.nn.sigmoid(gate_ff)
    silu_val = gate_ff * gate_sigma
    activation = (silu_val * up_val).astype(jnp.bfloat16)
    down_part = matmul_f32(activation, swiglu_full[2]).reshape(seq_count, full_len, model_width)
    ffn_branch = (
        lax.psum_scatter(down_part.astype(jnp.bfloat16), "ctx", scatter_dimension=1, tiled=True)
        .astype(jnp.float32)
        .reshape(local_rows, model_width)
    )
    layer_out = (hidden + ffn_branch).astype(jnp.bfloat16)
    domain_table = (
        domain_ids[:, None] == jnp.arange(domain_counts.shape[0], dtype=jnp.int32)[None, :]
    ).astype(jnp.float32)
    ratio = (
        domain_numer.astype(jnp.float32)
        / domain_denom.astype(jnp.float32)
        * LENGTH
        / domain_counts.astype(jnp.float32)
    )
    factor = jnp.sum(domain_table * ratio[None, :], 1)
    upstream = (cotangent.astype(jnp.float32) * factor[:, None, None]).reshape(
        local_rows, model_width
    )
    swiglu_back = swiglu_weights(swiglu_gate, swiglu_up, swiglu_down)
    out_low = upstream.astype(jnp.bfloat16)
    out_all = lax.all_gather(
        out_low.reshape(seq_count, local_len, model_width), "ctx", axis=1, tiled=True
    ).reshape(all_rows, model_width)
    dactivation = matmul_nt(out_all, swiglu_back[2])
    dgate_low = (dactivation * up_val * gate_sigma * (1.0 + gate_ff * (1.0 - gate_sigma))).astype(
        jnp.bfloat16
    )
    dup_low = (dactivation * silu_val).astype(jnp.bfloat16)
    grad_down = matmul_tn(activation, out_all)
    grad_gate = matmul_tn(normed_mid_all, dgate_low)
    grad_up = matmul_tn(normed_mid_all, dup_low)
    dmid_part = matmul_nt(dgate_low, swiglu_back[0]) + matmul_nt(dup_low, swiglu_back[1])
    dnormed_mid = lax.psum_scatter(
        dmid_part.reshape(seq_count, full_len, model_width), "ctx", scatter_dimension=1, tiled=True
    ).reshape(local_rows, model_width)
    grad_gain_mid = jnp.sum(dnormed_mid * hidden * inverse_mid, 0)
    dhidden = upstream + norm_back(dnormed_mid, hidden, inverse_mid, gain_mid)
    swiglu_grads = (
        lax.psum_scatter(
            grad_gate.astype(jnp.bfloat16), "dp", scatter_dimension=0, tiled=True
        ).astype(jnp.float32),
        lax.psum_scatter(
            grad_up.astype(jnp.bfloat16), "dp", scatter_dimension=0, tiled=True
        ).astype(jnp.float32),
        lax.psum_scatter(
            grad_down.astype(jnp.bfloat16), "dp", scatter_dimension=1, tiled=True
        ).astype(jnp.float32),
    )
    attn_back = attention_weights(query_proj, key_proj, value_proj, gating_proj, output_proj)
    dbranch_low = dhidden.astype(jnp.bfloat16)
    dbranch_all = lax.all_gather(
        dbranch_low.reshape(seq_count, local_len, model_width), "ctx", axis=1, tiled=True
    ).reshape(all_rows, model_width)
    grad_output = matmul_tn(mixed, dbranch_all)
    dmixed = matmul_nt(dbranch_all, attn_back[4])
    dattended_low = (dmixed * gate_sig).astype(jnp.bfloat16)
    dgating_low = (dmixed * attended * gate_sig * (1.0 - gate_sig)).astype(jnp.bfloat16)
    upstream_heads = dattended_low.reshape(seq_count, full_len, local_kv, group_size, head_dim)
    dquery_rot, dkey_rot, dvalue_sum = lax.map(
        lambda seq_items: softmax_backward(seq_items, causal),
        (query_groups, key_low, value_low, log_total, upstream_heads),
    )
    dvalue_low = dvalue_sum.reshape(all_rows, local_kv * head_dim).astype(jnp.bfloat16)
    dquery_normed = unrotate(
        dquery_rot.reshape(seq_count, full_len, local_heads, head_dim), cos_rows, sin_rows
    )
    dkey_normed = unrotate(
        dkey_rot.reshape(seq_count, full_len, local_kv, head_dim), cos_rows, sin_rows
    )
    grad_query_gain = jnp.sum(dquery_normed * query_raw * query_inv, (0, 1, 2))
    grad_key_gain = jnp.sum(dkey_normed * key_raw * key_inv, (0, 1, 2))
    dquery_low = (
        norm_back(dquery_normed, query_raw, query_inv, query_scale)
        .reshape(all_rows, -1)
        .astype(jnp.bfloat16)
    )
    dkey_low = (
        norm_back(dkey_normed, key_raw, key_inv, key_scale)
        .reshape(all_rows, -1)
        .astype(jnp.bfloat16)
    )
    dnormed_part = (
        matmul_nt(dquery_low, attn_back[0])
        + matmul_nt(dkey_low, attn_back[1])
        + matmul_nt(dvalue_low, attn_back[2])
        + matmul_nt(dgating_low, attn_back[3])
    )
    dnormed = (
        lax.psum_scatter(
            dnormed_part.reshape(seq_count, full_len, model_width).astype(jnp.bfloat16),
            "ctx",
            scatter_dimension=1,
            tiled=True,
        )
        .astype(jnp.float32)
        .reshape(local_rows, model_width)
    )
    grad_gain_in = jnp.sum(dnormed * inputs * inverse_in, 0)
    input_grad = (dhidden + norm_back(dnormed, inputs, inverse_in, gain_in)).astype(jnp.bfloat16)
    grad_query = matmul_tn(normed_all, dquery_low)
    grad_key = matmul_tn(normed_all, dkey_low)
    grad_value = matmul_tn(normed_all, dvalue_low)
    grad_gating = matmul_tn(normed_all, dgating_low)
    attention_grads = (
        lax.psum_scatter(
            grad_query.astype(jnp.bfloat16), "dp", scatter_dimension=0, tiled=True
        ).astype(jnp.float32),
        lax.psum_scatter(
            grad_key.astype(jnp.bfloat16), "dp", scatter_dimension=0, tiled=True
        ).astype(jnp.float32),
        lax.psum_scatter(
            grad_value.astype(jnp.bfloat16), "dp", scatter_dimension=0, tiled=True
        ).astype(jnp.float32),
        lax.psum_scatter(
            grad_gating.astype(jnp.bfloat16), "dp", scatter_dimension=0, tiled=True
        ).astype(jnp.float32),
        lax.psum_scatter(
            grad_output.astype(jnp.bfloat16), "dp", scatter_dimension=1, tiled=True
        ).astype(jnp.float32),
    )
    gain_grads = lax.psum(
        (grad_gain_in, grad_gain_mid, grad_query_gain, grad_key_gain), ("dp", "ctx")
    )
    return (
        layer_out.reshape(seq_count, local_len, model_width),
        input_grad.reshape(seq_count, local_len, model_width),
        gain_grads[0],
        gain_grads[2],
        gain_grads[3],
        attention_grads[0],
        attention_grads[1],
        attention_grads[2],
        attention_grads[3],
        attention_grads[4],
        gain_grads[1],
        swiglu_grads[0],
        swiglu_grads[1],
        swiglu_grads[2],
    )


def solution(mesh):
    return jax.shard_map(
        per_device,
        mesh=mesh,
        in_specs=(
            P("dp", "ctx", None),
            P("dp", "ctx", None),
            P("dp"),
            P(),
            P(),
            P(),
            P(),
            P(),
            P(),
            P("dp", "ctx"),
            P("dp", "ctx"),
            P("dp", "ctx"),
            P("dp", "ctx"),
            P("ctx", "dp"),
            P(),
            P("dp", "ctx"),
            P("dp", "ctx"),
            P("ctx", "dp"),
        ),
        out_specs=(
            P("dp", "ctx", None),
            P("dp", "ctx", None),
            P(),
            P(),
            P(),
            P("dp", "ctx"),
            P("dp", "ctx"),
            P("dp", "ctx"),
            P("dp", "ctx"),
            P("ctx", "dp"),
            P(),
            P("dp", "ctx"),
            P("dp", "ctx"),
            P("ctx", "dp"),
        ),
        check_vma=False,
    )
```

profile of v0, /device:TPU:0, one launch (start us, length us, event | category | flops | bytes accessed | tf_op | source)
XLA Modules:
  0.0 1734.3 jit_solution(1612069383806065240)
XLA Ops:
  18.6 34.5 %all-gather.17.cloned.1.call-done = bf16[2048,256]{1,0:T(8,128)(2,1)} async-done(((bf16[256,256]{1,0:T(8,128)(2,1)}), bf16[2048,256]{1,0:T(8,128)(2,1)}) %all-gather.17.cloned.1.call-update) | async-done | bytes 1048592 | tf_op jit(solution)/shard_map/all_gather | solution.py:64
  53.1 35.4 %all-gather.13.cloned.1.call-done = bf16[1,1024,2048]{2,1,0:T(8,128)(2,1)} async-done(((bf16[1,256,2048]{2,1,0:T(8,128)(2,1)}), bf16[1,1024,2048]{2,1,0:T(8,128)(2,1)}) %all-gather.13.cloned.1.call-update) | async-done | bytes 4194320 | tf_op jit(solution)/shard_map/all_gather | solution.py:163
  93.4 46.5 %all-gather.19.cloned.1.call-done = bf16[2048,512]{1,0:T(8,128)(2,1)} async-done(((bf16[256,512]{1,0:T(8,128)(2,1)}), bf16[2048,512]{1,0:T(8,128)(2,1)}) %all-gather.19.cloned.1.call-update) | async-done | bytes 2097168 | tf_op jit(solution)/shard_map/all_gather | solution.py:63
  162.1 18.5 %all-gather.15.cloned.1.call-done = bf16[2048,256]{1,0:T(8,128)(2,1)} async-done(((bf16[256,256]{1,0:T(8,128)(2,1)}), bf16[2048,256]{1,0:T(8,128)(2,1)}) %all-gather.15.cloned.1.call-update) | async-done | bytes 1048592 | tf_op jit(solution)/shard_map/all_gather | solution.py:65
  200.4 30.3 %all-gather.21.cloned.1.call-done = bf16[2048,512]{1,0:T(8,128)(2,1)} async-done(((bf16[256,512]{1,0:T(8,128)(2,1)}), bf16[2048,512]{1,0:T(8,128)(2,1)}) %all-gather.21.cloned.1.call-update) | async-done | bytes 2097168 | tf_op jit(solution)/shard_map/all_gather | solution.py:66
  237.5 44.6 %all-gather.23.cloned.1.call-done = bf16[512,2048]{1,0:T(8,128)(2,1)} async-done(((bf16[512,256]{1,0:T(8,128)(2,1)}), bf16[512,2048]{1,0:T(8,128)(2,1)}) %all-gather.23.cloned.1.call-update) | async-done | bytes 2097168 | tf_op jit(solution)/shard_map/all_gather | solution.py:67
  290.3 69.2 %reduce-scatter.13.cloned.1.call-done = f32[1,256,2048]{2,1,0:T(8,128)} async-done(((f32[1,1024,2048]{2,1,0:T(8,128)}), f32[1,256,2048]{2,1,0:T(8,128)}) %reduce-scatter.13.cloned.1.call-update) | async-done | bytes 2097168 | tf_op jit(solution)/shard_map/reduce_scatter | solution.py:191
  368.7 92.3 %all-gather.29.cloned.1.call-done = bf16[2048,1536]{1,0:T(8,128)(2,1)} async-done(((bf16[256,1536]{1,0:T(8,128)(2,1)}), bf16[2048,1536]{1,0:T(8,128)(2,1)}) %all-gather.29.cloned.1.call-update) | async-done | bytes 6291472 | tf_op jit(solution)/shard_map/all_gather | solution.py:74
  461.0 34.9 %all-gather.25.cloned.1.call-done = bf16[1,1024,2048]{2,1,0:T(8,128)(2,1)} async-done(((bf16[1,256,2048]{2,1,0:T(8,128)(2,1)}), bf16[1,1024,2048]{2,1,0:T(8,128)(2,1)}) %all-gather.25.cloned.1.call-update) | async-done | bytes 4194320 | tf_op jit(solution)/shard_map/all_gather | solution.py:198
  507.7 89.6 %all-gather.27.cloned.1.call-done = bf16[2048,1536]{1,0:T(8,128)(2,1)} async-done(((bf16[256,1536]{1,0:T(8,128)(2,1)}), bf16[2048,1536]{1,0:T(8,128)(2,1)}) %all-gather.27.cloned.1.call-update) | async-done | bytes 6291472 | tf_op jit(solution)/shard_map/all_gather | solution.py:73
  609.0 23.2 %all-gather.33.cloned.1.call-done = bf16[1,1024,2048]{2,1,0:T(8,128)(2,1)} async-done(((bf16[1,256,2048]{2,1,0:T(8,128)(2,1)}), bf16[1,1024,2048]{2,1,0:T(8,128)(2,1)}) %all-gather.33.cloned.1.call-update) | async-done | bytes 4194320 | tf_op jit(solution)/shard_map/all_gather | solution.py:229
  632.2 102.1 %all-gather.31.cloned.1.call-done = bf16[1536,2048]{1,0:T(8,128)(2,1)} async-done(((bf16[1536,256]{1,0:T(8,128)(2,1)}), bf16[1536,2048]{1,0:T(8,128)(2,1)}) %all-gather.31.cloned.1.call-update) | async-done | bytes 6291472 | tf_op jit(solution)/shard_map/all_gather | solution.py:75
  734.2 16.7 multiply_convert_fusion
  780.9 58.8 %reduce-scatter.17.cloned.1.call-done = f32[1,256,2048]{2,1,0:T(8,128)} async-done(((f32[1,1024,2048]{2,1,0:T(8,128)}), f32[1,256,2048]{2,1,0:T(8,128)}) %reduce-scatter.17.cloned.1.call-update) | async-done | bytes 2097168 | tf_op jit(solution)/shard_map/reduce_scatter | solution.py:241
  841.9 44.7 %reduce-scatter.15.cloned.1.call-done = bf16[1,256,2048]{2,1,0:T(8,128)(2,1)} async-done(((bf16[1,1024,2048]{2,1,0:T(8,128)(2,1)}), bf16[1,256,2048]{2,1,0:T(8,128)(2,1)}) %reduce-scatter.15.cloned.1.call-update) | async-done | bytes 1048592 | tf_op jit(solution)/shard_map/reduce_scatter | solution.py:209
  1051.7 118.6 %reduce-scatter.33.cloned.1.call-done = bf16[256,1536]{1,0:T(8,128)(2,1)} async-done(((bf16[2048,1536]{1,0:T(8,128)(2,1)}), bf16[256,1536]{1,0:T(8,128)(2,1)}) %reduce-scatter.33.cloned.1.call-update) | async-done | bytes 786448 | tf_op jit(solution)/shard_map/reduce_scatter | solution.py:250
  1172.8 118.5 %reduce-scatter.31.cloned.1.call-done = bf16[256,1536]{1,0:T(8,128)(2,1)} async-done(((bf16[2048,1536]{1,0:T(8,128)(2,1)}), bf16[256,1536]{1,0:T(8,128)(2,1)}) %reduce-scatter.31.cloned.1.call-update) | async-done | bytes 786448 | tf_op jit(solution)/shard_map/reduce_scatter | solution.py:247
  1293.8 63.9 %reduce-scatter.25.cloned.1.call-done = bf16[256,256]{1,0:T(8,128)(2,1)} async-done(((bf16[2048,256]{1,0:T(8,128)(2,1)}), bf16[256,256]{1,0:T(8,128)(2,1)}) %reduce-scatter.25.cloned.1.call-update) | async-done | bytes 131088 | tf_op jit(solution)/shard_map/reduce_scatter | solution.py:319
  1359.3 64.1 %reduce-scatter.23.cloned.1.call-done = bf16[256,256]{1,0:T(8,128)(2,1)} async-done(((bf16[2048,256]{1,0:T(8,128)(2,1)}), bf16[256,256]{1,0:T(8,128)(2,1)}) %reduce-scatter.23.cloned.1.call-update) | async-done | bytes 131088 | tf_op jit(solution)/shard_map/reduce_scatter | solution.py:316
  1425.1 69.7 %reduce-scatter.29.cloned.1.call-done = bf16[512,256]{1,0:T(8,128)(2,1)} async-done(((bf16[512,2048]{1,0:T(8,128)(2,1)}), bf16[512,256]{1,0:T(8,128)(2,1)}) %reduce-scatter.29.cloned.1.call-update) | async-done | bytes 262160 | tf_op jit(solution)/shard_map/reduce_scatter | solution.py:325
  1496.6 69.0 %reduce-scatter.27.cloned.1.call-done = bf16[256,512]{1,0:T(8,128)(2,1)} async-done(((bf16[2048,512]{1,0:T(8,128)(2,1)}), bf16[256,512]{1,0:T(8,128)(2,1)}) %reduce-scatter.27.cloned.1.call-update) | async-done | bytes 262160 | tf_op jit(solution)/shard_map/reduce_scatter | solution.py:322
  1567.4 69.1 %reduce-scatter.21.cloned.1.call-done = bf16[256,512]{1,0:T(8,128)(2,1)} async-done(((bf16[2048,512]{1,0:T(8,128)(2,1)}), bf16[256,512]{1,0:T(8,128)(2,1)}) %reduce-scatter.21.cloned.1.call-update) | async-done | bytes 262160 | tf_op jit(solution)/shard_map/reduce_scatter | solution.py:313
  1638.3 44.3 %reduce-scatter.19.cloned.1.call-done = bf16[1,256,2048]{2,1,0:T(8,128)(2,1)} async-done(((bf16[1,1024,2048]{2,1,0:T(8,128)(2,1)}), bf16[1,256,2048]{2,1,0:T(8,128)(2,1)}) %reduce-scatter.19.cloned.1.call-update) | async-done | bytes 1048592 | tf_op jit(solution)/shard_map/reduce_scatter | solution.py:297
  1684.4 39.8 %all-reduce = (f32[2048]{0:T(1024)}, f32[128]{0:T(128)}, f32[128]{0:T(128)}, f32[2048]{0:T(1024)}) all-reduce(f32[2048]{0:T(1024)S(1)} %get-tuple-element.57, f32[128]{0:T(128)S(1)} %bitcast_reduce_fusion, f32[128]{0:T(128)S(1)} %bitcast_reduce_fusion.1, f32[2048]{0:T(1024)S(1)} %get-tuple-element.55), channel_id=1, replica_groups=mesh['dp'=8,'ctx'=4] {'dp','ctx'}, use_global_device_ids=true, to_apply=%region_17.18 | all-reduce | flops 4352 | bytes 34816 | tf_op jit(solution)/shard_map/psum | solution.py:329
  (272 shorter events, 319.6 us)
Async XLA Ops:
  7.2 45.9 %all-gather.17.cloned.1.call-start = ((), (), s32[]{:S(2)}) async-start(), calls=%async_computation.14 | async-start | bytes 1179648 | tf_op jit(solution)/shard_map/all_gather | solution.py:64
  7.9 80.6 %all-gather.13.cloned.1.call-start = ((), (), s32[]{:S(2)}) async-start(), calls=%async_computation.12 | async-start | bytes 5242880 | tf_op jit(solution)/shard_map/all_gather | solution.py:163
  13.3 126.7 %all-gather.19.cloned.1.call-start = ((), (), s32[]{:S(2)}) async-start(), calls=%async_computation.15 | async-start | bytes 2359296 | tf_op jit(solution)/shard_map/all_gather | solution.py:63
  14.0 166.6 %all-gather.15.cloned.1.call-start = ((), (), s32[]{:S(2)}) async-start(), calls=%async_computation.13 | async-start | bytes 1179648 | tf_op jit(solution)/shard_map/all_gather | solution.py:65
  14.6 216.1 %all-gather.21.cloned.1.call-start = ((), (), s32[]{:S(2)}) async-start(), calls=%async_computation.16 | async-start | bytes 2359296 | tf_op jit(solution)/shard_map/all_gather | solution.py:66
  15.2 267.0 %all-gather.23.cloned.1.call-start = ((), (), s32[]{:S(2)}) async-start(), calls=%async_computation.17 | async-start | bytes 2359296 | tf_op jit(solution)/shard_map/all_gather | solution.py:67
  15.8 343.8 %reduce-scatter.13.cloned.1.call-start = ((), (), s32[]{:S(2)}) async-start(), calls=%async_computation.18 | async-start | bytes 10485760 | tf_op jit(solution)/shard_map/reduce_scatter | solution.py:191
  289.5 171.5 %all-gather.29.cloned.1.call-start = ((), (), s32[]{:S(2)}) async-start(), calls=%async_computation.21 | async-start | bytes 7077888 | tf_op jit(solution)/shard_map/all_gather | solution.py:74
  290.2 205.7 %all-gather.25.cloned.1.call-start = ((), (), s32[]{:S(2)}) async-start(), calls=%async_computation.19 | async-start | bytes 5242880 | tf_op jit(solution)/shard_map/all_gather | solution.py:198
  363.1 234.2 %all-gather.27.cloned.1.call-start = ((), (), s32[]{:S(2)}) async-start(), calls=%async_computation.20 | async-start | bytes 7077888 | tf_op jit(solution)/shard_map/all_gather | solution.py:73
  363.7 268.5 %all-gather.33.cloned.1.call-start = ((), (), s32[]{:S(2)}) async-start(), calls=%async_computation.24 | async-start | bytes 5242880 | tf_op jit(solution)/shard_map/all_gather | solution.py:229
  368.1 366.2 %all-gather.31.cloned.1.call-start = ((), (), s32[]{:S(2)}) async-start(), calls=%async_computation.22 | async-start | bytes 7077888 | tf_op jit(solution)/shard_map/all_gather | solution.py:75
  368.6 471.1 %reduce-scatter.17.cloned.1.call-start = ((), (), s32[]{:S(2)}) async-start(), calls=%async_computation.25 | async-start | bytes 10485760 | tf_op jit(solution)/shard_map/reduce_scatter | solution.py:241
  769.6 117.0 %reduce-scatter.15.cloned.1.call-start = ((), (), s32[]{:S(2)}) async-start(), calls=%async_computation.23 | async-start | bytes 5242880 | tf_op jit(solution)/shard_map/reduce_scatter | solution.py:209
  780.8 146.9 %all-gather.35.cloned.1.call-start = ((), (), s32[]{:S(2)}) async-start(), calls=%async_computation.26 | async-start | bytes 5242880 | tf_op jit(solution)/shard_map/all_gather | solution.py:259
  892.4 157.0 %reduce-scatter.35.cloned.1.call-start = ((), (), s32[]{:S(2)}) async-start(), calls=%async_computation.35 | async-start | bytes 7077888 | tf_op jit(solution)/shard_map/reduce_scatter | solution.py:253
  904.0 266.3 %reduce-scatter.33.cloned.1.call-start = ((), (), s32[]{:S(2)}) async-start(), calls=%async_computation.34 | async-start | bytes 7077888 | tf_op jit(solution)/shard_map/reduce_scatter | solution.py:250
  915.5 375.8 %reduce-scatter.31.cloned.1.call-start = ((), (), s32[]{:S(2)}) async-start(), calls=%async_computation.33 | async-start | bytes 7077888 | tf_op jit(solution)/shard_map/reduce_scatter | solution.py:247
  927.1 430.6 %reduce-scatter.25.cloned.1.call-start = ((), (), s32[]{:S(2)}) async-start(), calls=%async_computation.30 | async-start | bytes 1179648 | tf_op jit(solution)/shard_map/reduce_scatter | solution.py:319
  958.7 464.8 %reduce-scatter.23.cloned.1.call-start = ((), (), s32[]{:S(2)}) async-start(), calls=%async_computation.29 | async-start | bytes 1179648 | tf_op jit(solution)/shard_map/reduce_scatter | solution.py:316
  985.0 509.8 %reduce-scatter.29.cloned.1.call-start = ((), (), s32[]{:S(2)}) async-start(), calls=%async_computation.32 | async-start | bytes 2359296 | tf_op jit(solution)/shard_map/reduce_scatter | solution.py:325
  991.0 574.6 %reduce-scatter.27.cloned.1.call-start = ((), (), s32[]{:S(2)}) async-start(), calls=%async_computation.31 | async-start | bytes 2359296 | tf_op jit(solution)/shard_map/reduce_scatter | solution.py:322
  997.5 639.0 %reduce-scatter.21.cloned.1.call-start = ((), (), s32[]{:S(2)}) async-start(), calls=%async_computation.28 | async-start | bytes 2359296 | tf_op jit(solution)/shard_map/reduce_scatter | solution.py:313
  1011.6 670.9 %reduce-scatter.19.cloned.1.call-start = ((), (), s32[]{:S(2)}) async-start(), calls=%async_computation.27 | async-start | bytes 5242880 | tf_op jit(solution)/shard_map/reduce_scatter | solution.py:297
  (67 other events, 3181.3 us)
Sparse Core Ops, SparseCore 0:
  10.1 42.9 all-gather.16
  55.2 33.2 all-gather.12
  90.6 49.2 all-gather.18
  141.9 38.6 all-gather.14
  182.6 48.0 all-gather.20
  232.6 49.5 all-gather.22
  289.6 69.8 reduce-scatter.12
  361.9 99.0 all-gather.28
  463.2 32.6 all-gather.24
  498.2 99.0 all-gather.26
  599.5 32.6 all-gather.32
  634.3 99.9 all-gather.30
  769.8 69.9 reduce-scatter.16
  842.1 44.4 reduce-scatter.14
  892.5 34.4 all-gather.34
  930.9 118.3 reduce-scatter.34
  1053.2 117.0 reduce-scatter.32
  1174.2 117.0 reduce-scatter.30
  1295.1 62.5 reduce-scatter.24
  1361.0 62.4 reduce-scatter.22
  1427.4 67.3 reduce-scatter.28
  1498.7 66.7 reduce-scatter.26
  1569.5 66.9 reduce-scatter.20
  1639.0 43.4 reduce-scatter.18
where the time goes:
time: 1740 us; the launch traced here: 1730 us
  waiting for transfers between devices  1360 us (78%)
  matrix products  228 us (13%)
  other arithmetic  73.9 us (4%)
  blocking collectives  39.8 us (2%)
    reduce_scatter x1, waiting for transfers between devices, per_device(): lax.psum_scatter(grad_up.astype(jnp.bfloat16), 'dp', scatter_dimension=0,...  119 us
    reduce_scatter x1, waiting for transfers between devices, per_device(): lax.psum_scatter(grad_gate.astype(jnp.bfloat16), 'dp', scatter_dimension=...  119 us
    all_gather x1, waiting for transfers between devices, swiglu_weights(): lax.all_gather(swiglu_down, 'dp', axis=1, tiled=True)  102 us
    all_gather x1, waiting for transfers between devices, swiglu_weights(): lax.all_gather(swiglu_up, 'dp', axis=0, tiled=True)  92.3 us
    all_gather x1, waiting for transfers between devices, swiglu_weights(): lax.all_gather(swiglu_gate, 'dp', axis=0, tiled=True)  89.6 us
    reduce_scatter x1, waiting for transfers between devices, per_device(): lax.psum_scatter(grad_output.astype(jnp.bfloat16), 'dp', scatter_dimensio...  69.7 us
    reduce_scatter x1, waiting for transfers between devices, per_device(): lax.psum_scatter(branch_part, 'ctx', scatter_dimension=1, tiled=True)  69.2 us
    reduce_scatter x1, waiting for transfers between devices, per_device(): lax.psum_scatter(grad_query.astype(jnp.bfloat16), 'dp', scatter_dimension...  69.1 us
  transfers between devices with their start and end apart: 24, of which 23 were waited for; matrix products, arithmetic and copies ran while one was open for 15% of the time, Pallas kernels for 0%

commit v1 on v0

--- a/solution.py
+++ b/solution.py
@@ -1,35 +1,38 @@
+import functools
+
 import jax
 import jax.numpy as jnp
 from jax import lax
+from jax.experimental import pallas as pl
+from jax.experimental.pallas import tpu as pltpu
+from jax.sharding import Mesh
 from jax.sharding import PartitionSpec as P
 
 LENGTH = 1024
-
 
 EPSILON = 1e-06
 ROPE_BASE = 1000000.0
-
-
-def matmul_f32(left, right):
-    return jnp.dot(left, right, preferred_element_type=jnp.float32)
-
-
-def matmul_tn(left, right):
-    return lax.dot_general(
-        left, right, (((0,), (0,)), ((), ())), preferred_element_type=jnp.float32
-    )
-
-
-def matmul_nt(left, right):
-    return lax.dot_general(
-        left, right, (((1,), (1,)), ((), ())), preferred_element_type=jnp.float32
-    )
+MESH = pl.DeviceIdType.MESH
+BF16 = jnp.bfloat16
+F32 = jnp.float32
+
+
+def dot_nn(left, right):
+    return jnp.dot(left, right, preferred_element_type=F32)
+
+
+def dot_tn(left, right):
+    return lax.dot_general(left, right, (((0,), (0,)), ((), ())), preferred_element_type=F32)
+
+
+def dot_nt(left, right):
+    return lax.dot_general(left, right, (((1,), (1,)), ((), ())), preferred_element_type=F32)
 
 
 def rope_tables(positions, head_width):
     halfway = head_width // 2
-    inverse = 1.0 / ROPE_BASE ** (jnp.arange(halfway, dtype=jnp.float32) * (2.0 / head_width))
-    angles = positions.astype(jnp.float32)[:, None] * inverse[None, :]
+    inverse = 1.0 / ROPE_BASE ** (jnp.arange(halfway, dtype=F32) * (2.0 / head_width))
+    angles = positions.astype(F32)[:, None] * inverse[None, :]
     return (jnp.cos(angles), jnp.sin(angles))
 
 
@@ -56,6 +59,262 @@
     return inverse * scaled - values_in * (inverse * inverse * inverse) * jnp.mean(
         scaled * values_in, -1, keepdims=True
     )
+
+
+def greet(neighbours):
+    barrier = pltpu.get_barrier_semaphore()
+    for neighbour in neighbours:
+        pl.semaphore_signal(barrier, inc=1, device_id=neighbour, device_id_type=MESH)
+    pl.semaphore_wait(barrier, len(neighbours))
+
+
+def gather_kernel(rows, s_ref, out_ref, local_sem, send, recv):
+    y, x, c = lax.axis_index("y"), lax.axis_index("x"), lax.axis_index("c")
+    to_y, to_x, to_c = {"y": 1 - y}, {"x": 1 - x}, {"c": 1 - c}
+    greet((to_y, to_x, to_c))
+    half = rows // 2
+    low, high = pl.ds(0, half), pl.ds(half, half)
+
+    def remote(index, source, target, device):
+        return pltpu.make_async_remote_copy(
+            src_ref=source,
+            dst_ref=target,
+            send_sem=send.at[index],
+            recv_sem=recv.at[index],
+            device_id=device,
+            device_id_type=MESH,
+        )
+
+    mine = out_ref.at[y, x, c]
+    from_x = out_ref.at[y, 1 - x, c]
+    from_y = out_ref.at[1 - y, x, c]
+    diagonal = out_ref.at[1 - y, 1 - x, c]
+    x_low = remote(0, s_ref.at[low], mine.at[low], to_x)
+    y_high = remote(1, s_ref.at[high], mine.at[high], to_y)
+    x_high = remote(2, s_ref.at[high], mine.at[high], to_x)
+    y_low = remote(3, s_ref.at[low], mine.at[low], to_y)
+    c_own = remote(4, s_ref, mine, to_c)
+    local = pltpu.make_async_copy(s_ref, mine, local_sem)
+    for copy in (x_low, y_high, x_high, y_low, c_own, local):
+        copy.start()
+    x_low.wait_recv()
+    forward_y = remote(5, from_x.at[low], from_x.at[low], to_y)
+    forward_y.start()
+    y_high.wait_recv()
+    forward_x = remote(6, from_y.at[high], from_y.at[high], to_x)
+    forward_x.start()
+    x_high.wait_recv()
+    c_x = remote(7, from_x, from_x, to_c)
+    c_x.start()
+    y_low.wait_recv()
+    c_y = remote(8, from_y, from_y, to_c)
+    c_y.start()
+    forward_y.wait_recv()
+    c_low = remote(9, diagonal.at[low], diagonal.at[low], to_c)
+    c_low.start()
+    forward_x.wait_recv()
+    c_high = remote(10, diagonal.at[high], diagonal.at[high], to_c)
+    c_high.start()
+    for copy in (c_own, c_x, c_y, c_low, c_high):
+        copy.wait()
+    for copy in (x_low, y_high, x_high, y_low, forward_y, forward_x):
+        copy.wait_send()
+    local.wait()
+
+
+def gather_tokens(shard):
+    rows, width = shard.shape
+    return pl.pallas_call(
+        functools.partial(gather_kernel, rows),
+        out_shape=jax.ShapeDtypeStruct((2, 2, 2, rows, width), shard.dtype),
+        in_specs=[pl.BlockSpec(memory_space=pltpu.VMEM)],
+        out_specs=pl.BlockSpec(memory_space=pl.ANY),
+        scratch_shapes=[
+            pltpu.SemaphoreType.DMA,
+            pltpu.SemaphoreType.DMA((11,)),
+            pltpu.SemaphoreType.DMA((11,)),
+        ],
+        compiler_params=pltpu.CompilerParams(collective_id=0, has_side_effects=True),
+        name="gather_tokens",
+    )(shard).reshape(8 * rows, width)
+
+
+def scatter_kernel(rows, parts_ref, out_ref, own, got, x_diag, y_diag, x_got, y_got, load_sem, send, recv):
+    y, x, c = lax.axis_index("y"), lax.axis_index("x"), lax.axis_index("c")
+    to_y, to_x, to_c = {"y": 1 - y}, {"x": 1 - x}, {"c": 1 - c}
+    half = rows // 2
+    low, high = pl.ds(0, half), pl.ds(half, half)
+    targets = ((1 - y, 1 - x), (1 - y, x), (y, 1 - x), (y, x))
+    loads = [
+        pltpu.make_async_copy(parts_ref.at[a, b, c], own.at[i], load_sem.at[i])
+        for i, (a, b) in enumerate(targets)
+    ]
+    for load in loads:
+        load.start()
+    greet((to_y, to_x, to_c))
+
+    def remote(index, source, target, device):
+        return pltpu.make_async_remote_copy(
+            src_ref=source,
+            dst_ref=target,
+            send_sem=send.at[index],
+            recv_sem=recv.at[index],
+            device_id=device,
+            device_id_type=MESH,
+        )
+
+    crossing = [
+        remote(i, parts_ref.at[a, b, 1 - c], got.at[i], to_c) for i, (a, b) in enumerate(targets)
+    ]
+    for copy in crossing:
+        copy.start()
+    step = 64
+
+    def add_into(target, start, count, *others):
+        @pl.loop(0, count // step)
+        def _(i):
+            at = pl.ds(start + i * step, step)
+            total = target[at].astype(F32)
+            for other, base in others:
+                total = total + other[pl.ds(base + i * step, step)].astype(F32)
+            target[at] = total.astype(target.dtype)
+
+    def cores(i):
+        loads[i].wait()
+        crossing[i].wait_recv()
+        add_into(own.at[i], 0, rows, (got.at[i], 0))
+
+    cores(0)
+    diag_x = remote(4, own.at[0, low], x_diag, to_x)
+    diag_y = remote(5, own.at[0, high], y_diag, to_y)
+    diag_x.start()
+    diag_y.start()
+    cores(1)
+    y_high = remote(6, own.at[1, high], y_got.at[high], to_y)
+    y_high.start()
+    cores(2)
+    x_low = remote(7, own.at[2, low], x_got.at[low], to_x)
+    x_low.start()
+    cores(3)
+    diag_x.wait_recv()
+    add_into(own.at[1], 0, half, (x_diag, 0))
+    y_low = remote(8, own.at[1, low], y_got.at[low], to_y)
+    y_low.start()
+    diag_y.wait_recv()
+    add_into(own.at[2], half, half, (y_diag, 0))
+    x_high = remote(9, own.at[2, high], x_got.at[high], to_x)
+    x_high.start()
+    y_high.wait_recv()
+    x_low.wait_recv()
+    y_low.wait_recv()
+    x_high.wait_recv()
+
+    @pl.loop(0, rows // step)
+    def _(i):
+        at = pl.ds(i * step, step)
+        out_ref[at] = own[3, at].astype(F32) + x_got[at].astype(F32) + y_got[at].astype(F32)
+
+    for copy in (*crossing, diag_x, diag_y, y_high, x_low, y_low, x_high):
+        copy.wait_send()
+
+
+def scatter_tokens(parts):
+    rows, width = parts.shape[0] // 8, parts.shape[1]
+    return pl.pallas_call(
+        functools.partial(scatter_kernel, rows),
+        out_shape=jax.ShapeDtypeStruct((rows, width), F32),
+        in_specs=[pl.BlockSpec(memory_space=pl.ANY)],
+        out_specs=pl.BlockSpec(memory_space=pltpu.VMEM),
+        scratch_shapes=[
+            pltpu.VMEM((4, rows, width), parts.dtype),
+            pltpu.VMEM((4, rows, width), parts.dtype),
+            pltpu.VMEM((rows // 2, width), parts.dtype),
+            pltpu.VMEM((rows // 2, width), parts.dtype),
+            pltpu.VMEM((rows, width), parts.dtype),
+            pltpu.VMEM((rows, width), parts.dtype),
+            pltpu.SemaphoreType.DMA((4,)),
+            pltpu.SemaphoreType.DMA((10,)),
+            pltpu.SemaphoreType.DMA((10,)),
+        ],
+        compiler_params=pltpu.CompilerParams(collective_id=1, has_side_effects=True),
+        name="scatter_tokens",
+    )(parts.reshape(2, 2, 2, rows, width))
+
+
+def swap_y(value):
+    return lax.ppermute(value, "y", [(0, 1), (1, 0)])
+
+
+def in_y_order(mine, theirs, axis):
+    first = lax.axis_index("y") == 0
+    return jnp.where(
+        first, jnp.concatenate([mine, theirs], axis), jnp.concatenate([theirs, mine], axis)
+    )
+
+
+def column_half(weight, which):
+    half = weight.shape[1] // 2
+    return lax.dynamic_slice_in_dim(weight, which * half, half, 1)
+
+
+def pack_half(weights, which):
+    return jnp.concatenate([column_half(weight, which) for weight in weights], 1)
+
+
+def gather_weights(weights):
+    y = lax.axis_index("y")
+    mine, theirs = pack_half(weights, y), pack_half(weights, 1 - y)
+    rows = in_y_order(mine, swap_y(theirs), 0)
+    return lax.all_gather(rows, "z", axis=0, tiled=True)
+
+
+def scatter_grads(grad):
+    return lax.psum_scatter(grad.astype(BF16), "z", scatter_dimension=0, tiled=True)
+
+
+def finish_grads(part, widths):
+    y = lax.axis_index("y")
+    half = part.shape[0] // 2
+    mine = lax.dynamic_slice_in_dim(part, y * half, half, 0)
+    theirs = swap_y(lax.dynamic_slice_in_dim(part, (1 - y) * half, half, 0))
+    outs, start = [], 0
+    for width in widths:
+        piece = slice(start, start + width)
+        outs.append(in_y_order(mine[:, piece], theirs[:, piece], 1).astype(F32))
+        start += width
+    return outs
+
+
+def softmax_forward(queries, keys_seq, values_seq, causal):
+    scaling = queries.shape[-1] ** (-0.5)
+    scores = jnp.einsum("sqjd,skd->sjqk", queries, keys_seq, preferred_element_type=F32) * scaling
+    scores = jnp.where(causal, scores, -1e30)
+    highest = jnp.max(scores, -1, keepdims=True)
+    exp_vals = jnp.exp(scores - highest)
+    row_totals = jnp.sum(exp_vals, -1, keepdims=True)
+    attn_probs = (exp_vals / row_totals).astype(BF16)
+    attended = jnp.einsum("sjqk,skd->sqjd", attn_probs, values_seq, preferred_element_type=F32)
+    return (attended, highest[..., 0] + jnp.log(row_totals[..., 0]))
+
+
+def softmax_backward(queries, keys_seq, values_seq, log_total, upstream, causal):
+    scaling = queries.shape[-1] ** (-0.5)
+    scores = jnp.einsum("sqjd,skd->sjqk", queries, keys_seq, preferred_element_type=F32) * scaling
+    scores = jnp.where(causal, scores, -1e30)
+    attn_probs = jnp.exp(scores - log_total[..., None])
+    dprobs = jnp.einsum("sqjd,skd->sjqk", upstream, values_seq, preferred_element_type=F32)
+    centre = jnp.sum(dprobs * attn_probs, -1, keepdims=True)
+    dscores = (attn_probs * (dprobs - centre)).astype(BF16)
+    dqueries = (
+        jnp.einsum("sjqk,skd->sqjd", dscores, keys_seq, preferred_element_type=F32) * scaling
+    )
+    key_grads = (
+        jnp.einsum("sjqk,sqjd->skd", dscores, queries, preferred_element_type=F32) * scaling
+    )
+    value_grads = jnp.einsum(
+        "sjqk,sqjd->skd", attn_probs.astype(BF16), upstream, preferred_element_type=F32
+    )
+    return (dqueries, key_grads, value_grads)
 
 
 def attention_weights(query_proj, key_proj, value_proj, gating_proj, output_proj):
@@ -76,7 +335,7 @@
     )
 
 
-def softmax_forward(seq_items, causal):
+def softmax_forward_mapped(seq_items, causal):
     queries, keys_seq, values_seq = seq_items
     scaling = queries.shape[-1] ** (-0.5)
     scores = (
@@ -94,7 +353,7 @@
     return (attended, highest[..., 0] + jnp.log(row_totals[..., 0]))
 
 
-def softmax_backward(seq_items, causal):
+def softmax_backward_mapped(seq_items, causal):
     queries, keys_seq, values_seq, log_total, upstream = seq_items
     scaling = queries.shape[-1] ** (-0.5)
     scores = (
@@ -123,7 +382,7 @@
     return (dqueries, key_grads.reshape(key_rows, -1), value_grads.reshape(key_rows, -1))
 
 
-def per_device(
+def per_device_wide(
     tokens,
     cotangent,
     domain_ids,
@@ -164,16 +423,16 @@
         normed.reshape(seq_count, local_len, model_width), "ctx", axis=1, tiled=True
     ).reshape(all_rows, model_width)
     attn_full = attention_weights(query_proj, key_proj, value_proj, gating_proj, output_proj)
-    query_raw = matmul_f32(normed_all, attn_full[0]).reshape(
+    query_raw = dot_nn(normed_all, attn_full[0]).reshape(
         seq_count, full_len, local_heads, head_dim
     )
-    key_raw = matmul_f32(normed_all, attn_full[1]).reshape(seq_count, full_len, local_kv, head_dim)
+    key_raw = dot_nn(normed_all, attn_full[1]).reshape(seq_count, full_len, local_kv, head_dim)
     value_low = (
-        matmul_f32(normed_all, attn_full[2])
+        dot_nn(normed_all, attn_full[2])
         .astype(jnp.bfloat16)
         .reshape(seq_count, full_len, local_kv, head_dim)
     )
-    gate_pre = matmul_f32(normed_all, attn_full[3])
+    gate_pre = dot_nn(normed_all, attn_full[3])
     query_scale = query_gain.astype(jnp.float32)
     key_scale = key_gain.astype(jnp.float32)
     query_inv = lax.rsqrt(jnp.mean(query_raw * query_raw, -1, keepdims=True) + EPSILON)
@@ -182,12 +441,12 @@
     key_low = rotate(key_raw * key_inv * key_scale, cos_rows, sin_rows).astype(jnp.bfloat16)
     query_groups = query_low.reshape(seq_count, full_len, local_kv, group_size, head_dim)
     attended, log_total = lax.map(
-        lambda seq_items: softmax_forward(seq_items, causal), (query_groups, key_low, value_low)
+        lambda seq_items: softmax_forward_mapped(seq_items, causal), (query_groups, key_low, value_low)
     )
     attended = attended.reshape(all_rows, local_heads * head_dim)
     gate_sig = jax.nn.sigmoid(gate_pre)
     mixed = (attended * gate_sig).astype(jnp.bfloat16)
-    branch_part = matmul_f32(mixed, attn_full[4]).reshape(seq_count, full_len, model_width)
+    branch_part = dot_nn(mixed, attn_full[4]).reshape(seq_count, full_len, model_width)
     branch = lax.psum_scatter(branch_part, "ctx", scatter_dimension=1, tiled=True).reshape(
         local_rows, model_width
     )
@@ -199,12 +458,12 @@
         normed_mid.reshape(seq_count, local_len, model_width), "ctx", axis=1, tiled=True
     ).reshape(all_rows, model_width)
     swiglu_full = swiglu_weights(swiglu_gate, swiglu_up, swiglu_down)
-    gate_ff = matmul_f32(normed_mid_all, swiglu_full[0])
-    up_val = matmul_f32(normed_mid_all, swiglu_full[1])
+    gate_ff = dot_nn(normed_mid_all, swiglu_full[0])
+    up_val = dot_nn(normed_mid_all, swiglu_full[1])
     gate_sigma = jax.nn.sigmoid(gate_ff)
     silu_val = gate_ff * gate_sigma
     activation = (silu_val * up_val).astype(jnp.bfloat16)
-    down_part = matmul_f32(activation, swiglu_full[2]).reshape(seq_count, full_len, model_width)
+    down_part = dot_nn(activation, swiglu_full[2]).reshape(seq_count, full_len, model_width)
     ffn_branch = (
         lax.psum_scatter(down_part.astype(jnp.bfloat16), "ctx", scatter_dimension=1, tiled=True)
         .astype(jnp.float32)
@@ -229,15 +488,15 @@
     out_all = lax.all_gather(
         out_low.reshape(seq_count, local_len, model_width), "ctx", axis=1, tiled=True
     ).reshape(all_rows, model_width)
-    dactivation = matmul_nt(out_all, swiglu_back[2])
+    dactivation = dot_nt(out_all, swiglu_back[2])
     dgate_low = (dactivation * up_val * gate_sigma * (1.0 + gate_ff * (1.0 - gate_sigma))).astype(
         jnp.bfloat16
     )
     dup_low = (dactivation * silu_val).astype(jnp.bfloat16)
-    grad_down = matmul_tn(activation, out_all)
-    grad_gate = matmul_tn(normed_mid_all, dgate_low)
-    grad_up = matmul_tn(normed_mid_all, dup_low)
-    dmid_part = matmul_nt(dgate_low, swiglu_back[0]) + matmul_nt(dup_low, swiglu_back[1])
+    grad_down = dot_tn(activation, out_all)
+    grad_gate = dot_tn(normed_mid_all, dgate_low)
+    grad_up = dot_tn(normed_mid_all, dup_low)
+    dmid_part = dot_nt(dgate_low, swiglu_back[0]) + dot_nt(dup_low, swiglu_back[1])
     dnormed_mid = lax.psum_scatter(
         dmid_part.reshape(seq_count, full_len, model_width), "ctx", scatter_dimension=1, tiled=True
     ).reshape(local_rows, model_width)
@@ -259,13 +518,13 @@
     dbranch_all = lax.all_gather(
         dbranch_low.reshape(seq_count, local_len, model_width), "ctx", axis=1, tiled=True
     ).reshape(all_rows, model_width)
-    grad_output = matmul_tn(mixed, dbranch_all)
-    dmixed = matmul_nt(dbranch_all, attn_back[4])
+    grad_output = dot_tn(mixed, dbranch_all)
+    dmixed = dot_nt(dbranch_all, attn_back[4])
     dattended_low = (dmixed * gate_sig).astype(jnp.bfloat16)
     dgating_low = (dmixed * attended * gate_sig * (1.0 - gate_sig)).astype(jnp.bfloat16)
     upstream_heads = dattended_low.reshape(seq_count, full_len, local_kv, group_size, head_dim)
     dquery_rot, dkey_rot, dvalue_sum = lax.map(
-        lambda seq_items: softmax_backward(seq_items, causal),
+        lambda seq_items: softmax_backward_mapped(seq_items, causal),
         (query_groups, key_low, value_low, log_total, upstream_heads),
     )
     dvalue_low = dvalue_sum.reshape(all_rows, local_kv * head_dim).astype(jnp.bfloat16)
@@ -288,10 +547,10 @@
         .astype(jnp.bfloat16)
     )
     dnormed_part = (
-        matmul_nt(dquery_low, attn_back[0])
-        + matmul_nt(dkey_low, attn_back[1])
-        + matmul_nt(dvalue_low, attn_back[2])
-        + matmul_nt(dgating_low, attn_back[3])
+        dot_nt(dquery_low, attn_back[0])
+        + dot_nt(dkey_low, attn_back[1])
+        + dot_nt(dvalue_low, attn_back[2])
+        + dot_nt(dgating_low, attn_back[3])
     )
     dnormed = (
         lax.psum_scatter(
@@ -305,10 +564,10 @@
     )
     grad_gain_in = jnp.sum(dnormed * inputs * inverse_in, 0)
     input_grad = (dhidden + norm_back(dnormed, inputs, inverse_in, gain_in)).astype(jnp.bfloat16)
-    grad_query = matmul_tn(normed_all, dquery_low)
-    grad_key = matmul_tn(normed_all, dkey_low)
-    grad_value = matmul_tn(normed_all, dvalue_low)
-    grad_gating = matmul_tn(normed_all, dgating_low)
+    grad_query = dot_tn(normed_all, dquery_low)
+    grad_key = dot_tn(normed_all, dkey_low)
+    grad_value = dot_tn(normed_all, dvalue_low)
+    grad_gating = dot_tn(normed_all, dgating_low)
     attention_grads = (
         lax.psum_scatter(
             grad_query.astype(jnp.bfloat16), "dp", scatter_dimension=0, tiled=True
@@ -347,45 +606,176 @@
     )
 
 
+def per_device(
+    tokens,
+    cotangent,
+    domain_ids,
+    domain_counts,
+    domain_numer,
+    domain_denom,
+    attention_gain,
+    query_gain,
+    key_gain,
+    query_proj,
+    key_proj,
+    value_proj,
+    gating_proj,
+    output_proj,
+    swiglu_gain,
+    swiglu_gate,
+    swiglu_up,
+    swiglu_down,
+):
+    seq_count, local_len, width = tokens.shape
+    rows = seq_count * local_len
+    full_len = local_len * lax.axis_size("x") * lax.axis_size("c")
+    seqs = seq_count * lax.axis_size("y")
+    head = query_gain.shape[0]
+    kv_cols = key_proj.shape[1] // 2
+    q_cols = query_proj.shape[1] // 2
+    ff_cols = swiglu_gate.shape[1] // 2
+    heads = q_cols // head
+    positions = jnp.arange(full_len, dtype=jnp.int32)
+    causal = positions[:, None] >= positions[None, :]
+    cosine, sine = rope_tables(positions, head)
+    cos_rows, sin_rows = cosine[:, None, :], sine[:, None, :]
+
+    inputs = tokens.reshape(rows, width).astype(F32)
+    inverse_in = lax.rsqrt(jnp.mean(inputs * inputs, -1, keepdims=True) + EPSILON)
+    gain_in = attention_gain.astype(F32)
+    normed = (inputs * inverse_in * gain_in).astype(BF16)
+
+    w_qkv = gather_weights((query_proj, key_proj, value_proj))
+    normed_all = gather_tokens(normed)
+    gating_proj, output_t, normed_all = lax.optimization_barrier(
+        (gating_proj, output_proj.T, normed_all)
+    )
+    w_go = gather_weights((gating_proj, output_t))
+    w_gu = gather_weights((swiglu_gate, swiglu_up))
+    w_dt = gather_weights((swiglu_down.T,))
+
+    domain_table = (
+        domain_ids[:, None] == jnp.arange(domain_counts.shape[0], dtype=jnp.int32)[None, :]
+    ).astype(F32)
+    ratio = (
+        domain_numer.astype(F32) / domain_denom.astype(F32) * LENGTH / domain_counts.astype(F32)
+    )
+    factor = jnp.sum(domain_table * ratio[None, :], 1)
+    upstream = (cotangent.astype(F32) * factor[:, None, None]).reshape(rows, width)
+    out_low = upstream.astype(BF16)
+    out_all = gather_tokens(out_low)
+
+    qkv = dot_nn(normed_all, w_qkv)
+    query_raw = qkv[:, :q_cols].reshape(seqs, full_len, heads, head)
+    key_raw = qkv[:, q_cols : q_cols + kv_cols].reshape(seqs, full_len, 1, head)
+    value_low = qkv[:, q_cols + kv_cols :].astype(BF16).reshape(seqs, full_len, head)
+    query_scale, key_scale = query_gain.astype(F32), key_gain.astype(F32)
+    query_inv = lax.rsqrt(jnp.mean(query_raw * query_raw, -1, keepdims=True) + EPSILON)
+    key_inv = lax.rsqrt(jnp.mean(key_raw * key_raw, -1, keepdims=True) + EPSILON)
+    query_low = rotate(query_raw * query_inv * query_scale, cos_rows, sin_rows).astype(BF16)
+    key_low = rotate(key_raw * key_inv * key_scale, cos_rows, sin_rows).astype(BF16)
+    key_low = key_low.reshape(seqs, full_len, head)
+    attended, log_total = softmax_forward(query_low, key_low, value_low, causal)
+    attended = attended.reshape(seqs * full_len, q_cols)
+
+    w_g, w_ot = w_go[:, :q_cols], w_go[:, q_cols:]
+    gate_sig = jax.nn.sigmoid(dot_nn(normed_all, w_g))
+    mixed = (attended * gate_sig).astype(BF16)
+    branch = scatter_tokens(dot_nt(mixed, w_ot).astype(BF16))
+    hidden = inputs + branch
+    inverse_mid = lax.rsqrt(jnp.mean(hidden * hidden, -1, keepdims=True) + EPSILON)
+    gain_mid = swiglu_gain.astype(F32)
+    normed_mid = (hidden * inverse_mid * gain_mid).astype(BF16)
+    mid_all = gather_tokens(normed_mid)
+
+    gate_up = dot_nn(mid_all, w_gu)
+    gate_ff, up_val = gate_up[:, :ff_cols], gate_up[:, ff_cols:]
+    sigma = jax.nn.sigmoid(gate_ff)
+    silu = gate_ff * sigma
+    activation = (silu * up_val).astype(BF16)
+    part_dt = scatter_grads(dot_tn(out_all, activation))
+
+    dact = dot_nn(out_all, w_dt)
+    dgate = (dact * up_val * sigma * (1.0 + gate_ff * (1.0 - sigma))).astype(BF16)
+    dup = (dact * silu).astype(BF16)
+    dgu = jnp.concatenate([dgate, dup], 1)
+    dnormed_mid = scatter_tokens(dot_nt(dgu, w_gu).astype(BF16))
+    part_gu = scatter_grads(dot_tn(mid_all, dgu))
+    grad_gain_mid = jnp.sum(dnormed_mid * hidden * inverse_mid, 0)
+    dhidden = upstream + norm_back(dnormed_mid, hidden, inverse_mid, gain_mid)
+    dbranch_all = gather_tokens(dhidden.astype(BF16))
+
+    ffn_branch = scatter_tokens(dot_nt(activation, w_dt).astype(BF16))
+    layer_out = (hidden + ffn_branch).astype(BF16)
+
+    grad_ot = dot_tn(dbranch_all, mixed)
+    dmixed = dot_nn(dbranch_all, w_ot)
+    dattended = (dmixed * gate_sig).astype(BF16)
+    dgating = (dmixed * attended * gate_sig * (1.0 - gate_sig)).astype(BF16)
+    grad_g = dot_tn(normed_all, dgating)
+    part_go = scatter_grads(jnp.concatenate([grad_g.astype(BF16), grad_ot.astype(BF16)], 1))
+    dquery_rot, dkey_rot, dvalue_sum = softmax_backward(
+        query_low,
+        key_low,
+        value_low,
+        log_total,
+        dattended.reshape(seqs, full_len, heads, head),
+        causal,
+    )
+    dvalue = dvalue_sum.reshape(seqs * full_len, head).astype(BF16)
+    dquery_n = unrotate(dquery_rot, cos_rows, sin_rows)
+    dkey_n = unrotate(dkey_rot.reshape(seqs, full_len, 1, head), cos_rows, sin_rows)
+    grad_query_gain = jnp.sum(dquery_n * query_raw * query_inv, (0, 1, 2))
+    grad_key_gain = jnp.sum(dkey_n * key_raw * key_inv, (0, 1, 2))
+    dquery = norm_back(dquery_n, query_raw, query_inv, query_scale).astype(BF16)
+    dkey = norm_back(dkey_n, key_raw, key_inv, key_scale).astype(BF16)
+    dqkv = jnp.concatenate(
+        [dquery.reshape(seqs * full_len, -1), dkey.reshape(seqs * full_len, -1), dvalue], 1
+    )
+    part_qkv = scatter_grads(dot_tn(normed_all, dqkv))
+    dnormed = scatter_tokens((dot_nt(dqkv, w_qkv) + dot_nt(dgating, w_g)).astype(BF16))
+    grad_gain_in = jnp.sum(dnormed * inputs * inverse_in, 0)
+    input_grad = (dhidden + norm_back(dnormed, inputs, inverse_in, gain_in)).astype(BF16)
+
+    grad_down_t = finish_grads(part_dt, (ff_cols,))[0]
+    grad_gate, grad_up = finish_grads(part_gu, (ff_cols, ff_cols))
+    grad_gating, grad_output_t = finish_grads(part_go, (q_cols, q_cols))
+    grad_query, grad_key, grad_value = finish_grads(part_qkv, (q_cols, kv_cols, kv_cols))
+    gain_grads = lax.psum(
+        (grad_gain_in, grad_gain_mid, grad_query_gain, grad_key_gain), ("z", "y", "x", "c")
+    )
+    shape = (seq_count, local_len, width)
+    return (
+        layer_out.reshape(shape),
+        input_grad.reshape(shape),
+        gain_grads[0],
+        gain_grads[2],
+        gain_grads[3],
+        grad_query,
+        grad_key,
+        grad_value,
+        grad_gating,
+        grad_output_t.T,
+        gain_grads[1],
+        grad_gate,
+        grad_up,
+        grad_down_t.T,
+    )
+
+
 def solution(mesh):
+    if (mesh.shape["dp"], mesh.shape["ctx"]) == (8, 4):
+        body = per_device
+        mesh = Mesh(mesh.devices.reshape(4, 2, 2, 2), ("z", "y", "x", "c"))
+        dp, ctx = ("z", "y"), ("x", "c")
+    else:
+        body = per_device_wide
+        dp, ctx = "dp", "ctx"
+    tokens, weight, turned = P(dp, ctx, None), P(dp, ctx), P(ctx, dp)
     return jax.shard_map(
-        per_device,
+        body,
         mesh=mesh,
-        in_specs=(
-            P("dp", "ctx", None),
-            P("dp", "ctx", None),
-            P("dp"),
-            P(),
-            P(),
-            P(),
-            P(),
-            P(),
-            P(),
-            P("dp", "ctx"),
-            P("dp", "ctx"),
-            P("dp", "ctx"),
-            P("dp", "ctx"),
-            P("ctx", "dp"),
-            P(),
-            P("dp", "ctx"),
-            P("dp", "ctx"),
-            P("ctx", "dp"),
-        ),
-        out_specs=(
-            P("dp", "ctx", None),
-            P("dp", "ctx", None),
-            P(),
-            P(),
-            P(),
-            P("dp", "ctx"),
-            P("dp", "ctx"),
-            P("dp", "ctx"),
-            P("dp", "ctx"),
-            P("ctx", "dp"),
-            P(),
-            P("dp", "ctx"),
-            P("dp", "ctx"),
-            P("ctx", "dp"),
-        ),
+        in_specs=(tokens, tokens, P(dp), *[P()] * 6, *[weight] * 4, turned, P(), weight, weight, turned),
+        out_specs=(tokens, tokens, *[P()] * 3, *[weight] * 4, turned, P(), weight, weight, turned),
         check_vma=False,
     )

time: 1740 us -> 847 us (0.49)
  waiting for transfers between devices: 1360 us -> 116 us
  Pallas kernels: 0 us -> 330 us
  local copies, waits for them, and re-layouts: 13.1 us -> 51.9 us
  matrix products: 228 us -> 201 us
    reduce_scatter x12 -> x4, waiting for transfers between devices: 805 us -> 64.9 us  [scatter_grads(): lax.psum_scatter(grad.astype(BF16), 'z', scatter_dimension=0, tiled=True)]
    all_gather x12 -> x4, waiting for transfers between devices: 552 us -> 0.06 us  [gather_weights(): return lax.all_gather(rows, 'z', axis=0, tiled=True)]
    pallas_call x0 -> x8, Pallas kernels: none -> 330 us  [the longest x4 167 us: scatter_tokens(): pl.pallas_call(functools.partial(scatter_kernel, rows), out_shape=jax.Sha...]
    ppermute x0 -> x8, waiting for transfers between devices: none -> 51.4 us  [swap_y(): return lax.ppermute(value, 'y', [(0, 1), (1, 0)])]
    dot_general x30 -> x21, matrix products: 228 us -> 201 us  [the longest x5 57.3 us: dot_nn(): return jnp.dot(left, right, preferred_element_type=F32)]
    convert_element_type x19 -> x17, other arithmetic: 45.5 us -> 24.2 us  [the longest x1 8.52 us: softmax_backward(): dscores = (attn_probs * (dprobs - centre)).astype(BF16)]
  transfers between devices with their start and end apart: 24 -> 16, of which waited for: 23 -> 7; matrix products, arithmetic and copies ran while one was open for 15% -> 25% of each run, Pallas kernels for 0% -> 25%
where the time goes in v1:
time: 847 us; the launch traced here: 842 us
  Pallas kernels  330 us (39%)
  matrix products  201 us (24%)
  waiting for transfers between devices  116 us (14%)
  other arithmetic  72.6 us (9%)
  local copies, waits for them, and re-layouts  51.9 us (6%)
  blocking collectives  42.3 us (5%)
  between operations  16.2 us (2%)
  starting transfers between devices  11.3 us (1%)
    pallas_call x4, Pallas kernels, scatter_tokens(): pl.pallas_call(functools.partial(scatter_kernel, rows), out_shape=jax.Sha...  167 us
    pallas_call x4, Pallas kernels, gather_tokens(): pl.pallas_call(functools.partial(gather_kernel, rows), out_shape=jax.Shap...  163 us
    reduce_scatter x4, waiting for transfers between devices, scatter_grads(): lax.psum_scatter(grad.astype(BF16), 'z', scatter_dimension=0, tiled=True)  64.9 us
    dot_general x5, matrix products, dot_nn(): return jnp.dot(left, right, preferred_element_type=F32)  57.3 us
    dot_general x5, matrix products, dot_nt(): lax.dot_general(left, right, (((1,), (1,)), ((), ())), preferred_element_...  53 us
    ppermute x8, waiting for transfers between devices, swap_y(): return lax.ppermute(value, 'y', [(0, 1), (1, 0)])  51.4 us
    dot_general x5, matrix products, dot_tn(): lax.dot_general(left, right, (((0,), (0,)), ((), ())), preferred_element_...  46.2 us
    psum x1, blocking collectives, per_device(): lax.psum((grad_gain_in, grad_gain_mid, grad_query_gain, grad_key_gain), (...  42.3 us
  transfers between devices with their start and end apart: 16, of which 7 were waited for; matrix products, arithmetic and copies ran while one was open for 25% of the time, Pallas kernels for 25%

profile of v1, /device:TPU:0, one launch (start us, length us, event | category | flops | bytes accessed | tf_op | source)
XLA Modules:
  0.0 841.7 jit_solution(10122080806708627687)
XLA Ops:
  22.8 41.0 %gather_tokens.4 = bf16[2,2,2,256,2048]{4,3,2,1,0:T(8,128)(2,1)} custom-call(bf16[256,2048]{1,0:T(8,128)(2,1)} %fusion.15.s_ref), custom_call_target="tpu_custom_call" | custom-call | tf_op jit(solution)/shard_map/gather_tokens/pallas_call | solution.py:127
  74.8 18.3 %collective-permute-done.2 = bf16[256,1536]{1,0:T(8,128)(2,1)S(1)} collective-permute-done((bf16[256,1536]{1,0:T(8,128)(2,1)S(1)}, bf16[256,1536]{1,0:T(8,128)(2,1)S(1)}, u32[]{:S(2)}, u32[]{:S(2)}) %collective-permute-start.2) | collective-permute-done | bytes 786464 | tf_op jit(solution)/shard_map/ppermute | solution.py:245
  102.0 40.6 %gather_tokens.6 = bf16[2,2,2,256,2048]{4,3,2,1,0:T(8,128)(2,1)} custom-call(bf16[256,2048]{1,0:T(8,128)(2,1)} %bitcast_convert_fusion.s_ref), custom_call_target="tpu_custom_call" | custom-call | tf_op jit(solution)/shard_map/gather_tokens/pallas_call | solution.py:127
  175.2 8.2 fusion.75
  191.7 8.9 %fusion.32 = f32[2,1024,2,128]{1,3,2,0:T(8,128)} fusion(bf16[2,1024,128,1]{2,1,3,0:T(8,128)(2,1)S(1)} %bitcast.193, f32[2,2,1024,1024]{2,3,1,0:T(8,128)} %get-tuple-element.179, f32[2,2,1024]{2,1,0:T(2,128)S(1)} %fusion.3, f32[2,2,1024]{2,1,0:T(2,128)S(1)} %get-tuple-element.178), kind=kOutput, calls=%fused_computation.85 | convolution fusion | flops 1086324736 | bytes 19431424 | tf_op jit(solution)/shard_map/sjqk,skd->sqjd/dot_general | solution.py:296
  203.4 8.4 fusion.28
  217.5 41.6 %scatter_tokens.4 = f32[256,2048]{1,0:T(8,128)} custom-call(bf16[2,2,2,256,2048]{4,3,2,1,0:T(8,128)(2,1)} %bitcast.166), custom_call_target="tpu_custom_call" | custom-call | tf_op jit(solution)/shard_map/scatter_tokens/pallas_call | solution.py:223
  262.3 40.7 %gather_tokens.5 = bf16[2,2,2,256,2048]{4,3,2,1,0:T(8,128)(2,1)} custom-call(bf16[256,2048]{1,0:T(8,128)(2,1)} %multiply_convert_fusion.4.s_ref), custom_call_target="tpu_custom_call" | custom-call | tf_op jit(solution)/shard_map/gather_tokens/pallas_call | solution.py:127
  304.5 19.2 %fusion.77 = f32[2048,1536]{0,1:T(8,128)} fusion(bf16[2048,2048]{1,0:T(8,128)(2,1)} %bitcast.184, bf16[2048,1536]{1,0:T(8,128)(2,1)} %all-gather.9.cloned.1.call-done), kind=kOutput, calls=%fused_computation.202 | convolution fusion | flops 12884901888 | bytes 27262976 | tf_op jit(solution)/shard_map/dot_general | solution.py:21
  323.7 18.1 %multiply_convert_fusion.1 = (bf16[2048,768]{0,1:T(8,128)(2,1)}, bf16[2048,768]{0,1:T(8,128)(2,1)}, bf16[2048,768]{0,1:T(8,128)(2,1)S(1)}) fusion(f32[2048,1536]{0,1:T(8,128)} %fusion.77, bf16[2048,2048]{1,0:T(8,128)(2,1)} %bitcast.182, bf16[2048,768]{0,1:T(8,128)(2,1)} %all-gather.11.cloned.1.call-done), kind=kOutput, calls=%fused_computation.21 | convolution fusion | flops 6466043904 | bytes 33554432 | tf_op jit(solution)/shard_map/dot_general | solution.py:21
  341.9 9.2 %convolution_convert_fusion.1 = bf16[2048,2048]{1,0:T(8,128)(2,1)} fusion(bf16[2048,768]{0,1:T(8,128)(2,1)S(1)} %get-tuple-element.122, bf16[2048,768]{0,1:T(8,128)(2,1)S(1)} %copy-done.70), kind=kOutput, calls=%fused_computation.16 | convolution fusion | flops 6446645248 | bytes 14680064 | tf_op jit(solution)/shard_map/dot_general | solution.py:29
  351.0 41.6 %scatter_tokens.5 = f32[256,2048]{1,0:T(8,128)} custom-call(bf16[2,2,2,256,2048]{4,3,2,1,0:T(8,128)(2,1)} %bitcast.172), custom_call_target="tpu_custom_call" | custom-call | tf_op jit(solution)/shard_map/scatter_tokens/pallas_call | solution.py:223
  392.6 19.6 %convolution_convert_fusion = bf16[2048,2048]{1,0:T(8,128)(2,1)} fusion(bf16[2048,1536]{1,0:T(8,128)(2,1)} %all-gather.9.cloned.1.call-done, bf16[2048,768]{0,1:T(8,128)(2,1)} %get-tuple-element.121, bf16[2048,768]{0,1:T(8,128)(2,1)} %get-tuple-element.120), kind=kOutput, calls=%fused_computation.15 | convolution fusion | flops 12901679104 | bytes 20971520 | tf_op jit(solution)/shard_map/dot_general | solution.py:29
  412.3 41.5 %scatter_tokens.6 = f32[256,2048]{1,0:T(8,128)} custom-call(bf16[2,2,2,256,2048]{4,3,2,1,0:T(8,128)(2,1)} %bitcast.173), custom_call_target="tpu_custom_call" | custom-call | tf_op jit(solution)/shard_map/scatter_tokens/pallas_call | solution.py:223
  460.3 40.7 %gather_tokens.7 = bf16[2,2,2,256,2048]{4,3,2,1,0:T(8,128)(2,1)} custom-call(bf16[256,2048]{1,0:T(8,128)(2,1)} %get-tuple-element.116.s_ref), custom_call_target="tpu_custom_call" | custom-call | tf_op jit(solution)/shard_map/gather_tokens/pallas_call | solution.py:127
  521.8 8.5 %fusion.2 = bf16[2,2,1024,1024]{2,3,1,0:T(8,128)(2,1)S(1)} fusion(f32[2,1024,1024,2]{2,1,3,0:T(8,128)S(1)} %get-tuple-element.183, f32[2,2,1024,1024]{2,3,1,0:T(8,128)} %get-tuple-element.179, f32[2,2,1024]{2,1,0:T(2,128)S(1)} %get-tuple-element.182, f32[2,2,1024]{2,1,0:T(2,128)S(1)} %log_add_fusion), kind=kLoop, calls=%fused_computation.4 | loop fusion | flops 16777216 | bytes 41975808 | tf_op jit(solution)/shard_map/convert_element_type | solution.py:307
  568.1 9.8 %fusion.38 = bf16[2,1024,128]{2,1,0:T(8,128)(2,1)} fusion(f32[2,2,1024,1024]{2,3,1,0:T(8,128)} %get-tuple-element.179, f32[2,2,1024]{2,1,0:T(2,128)S(1)} %log_add_fusion, bf16[2,1024,2,128]{3,2,1,0:T(2,128)(2,1)S(1)} %copy-done.14), kind=kOutput, calls=%fused_computation.92 | convolution fusion | flops 1082392576 | bytes 18366464 | tf_op jit(solution)/shard_map/sjqk,sqjd->skd/dot_general | solution.py:314
  584.8 11.4 %convolution_convert_fusion.4 = bf16[2048,768]{1,0:T(8,128)(2,1)} fusion(bf16[2048,2048]{1,0:T(8,128)(2,1)} %bitcast.183, bf16[2048,768]{0,1:T(8,128)(2,1)} %copy-done.75), kind=kOutput, calls=%fused_computation.32 | convolution fusion | flops 6444023808 | bytes 14680064 | tf_op jit(solution)/shard_map/dot_general | solution.py:25
  598.0 18.4 %convolution_convert_fusion.3 = bf16[2048,1536]{1,0:T(8,128)(2,1)} fusion(bf16[2048,2048]{1,0:T(8,128)(2,1)} %bitcast.185, bf16[2048,768]{0,1:T(8,128)(2,1)} %get-tuple-element.121, bf16[2048,768]{0,1:T(8,128)(2,1)S(1)} %copy-done.76), kind=kOutput, calls=%fused_computation.18 | convolution fusion | flops 12900630528 | bytes 20971520 | tf_op jit(solution)/shard_map/dot_general | solution.py:25
  626.5 10.3 %add_convert_fusion = bf16[2048,2048]{1,0:T(8,128)(2,1)} fusion(f32[2048,2048]{1,0:T(8,128)} %fusion.46, bf16[2048,512]{0,1:T(8,128)(2,1)S(1)} %copy-done.71, bf16[2048,128]{1,0:T(8,128)(2,1)S(1)} %bitcast.198, bf16[2048,128]{1,0:T(8,128)(2,1)S(1)} %copy-done.47, bf16[2048,256]{1,0:T(8,128)(2,1)S(1)} %copy-done.41), kind=kOutput, calls=%fused_computation.6 | convolution fusion | flops 4309647360 | bytes 29360128 | tf_op jit(solution)/shard_map/dot_general | solution.py:29
  636.9 42.5 %scatter_tokens.7 = f32[256,2048]{1,0:T(8,128)} custom-call(bf16[2,2,2,256,2048]{4,3,2,1,0:T(8,128)(2,1)} %bitcast.171), custom_call_target="tpu_custom_call" | custom-call | tf_op jit(solution)/shard_map/scatter_tokens/pallas_call | solution.py:223
  681.7 42.3 %all-reduce = (f32[2048]{0:T(1024)}, f32[128]{0:T(128)}, f32[128]{0:T(128)}, f32[2048]{0:T(1024)}) all-reduce(f32[2048]{0:T(1024)S(1)} %get-tuple-element.108, f32[128]{0:T(128)S(1)} %bitcast_reduce_fusion, f32[128]{0:T(128)S(1)} %get-tuple-element.104, ...), channel_id=1, replica_groups=mesh['z'=4,'y'=2,'x'=2,'c'=2] {'z','y','x','c'}, use_global_device_ids=true, to_apply=%region_13.14 | all-reduce | flops 4352 | bytes 34816 | tf_op jit(solution)/shard_map/psum | solution.py:744
  744.2 64.8 %reduce-scatter.9.cloned.1.call-done = bf16[512,1536]{1,0:T(8,128)(2,1)} async-done(((bf16[2048,1536]{1,0:T(8,128)(2,1)}), bf16[512,1536]{1,0:T(8,128)(2,1)}) %reduce-scatter.9.cloned.1.call-update) | async-done | bytes 1572880 | tf_op jit(solution)/shard_map/reduce_scatter | solution.py:272
  818.8 12.0 %collective-permute-done.6 = bf16[256,1536]{1,0:T(8,128)(2,1)} collective-permute-done((bf16[256,1536]{1,0:T(8,128)(2,1)}, bf16[256,1536]{1,0:T(8,128)(2,1)}, u32[]{:S(2)}, u32[]{:S(2)}) %collective-permute-start.6) | collective-permute-done | bytes 786464 | tf_op jit(solution)/shard_map/ppermute | solution.py:245
  (309 shorter events, 207.9 us)
Async XLA Ops:
  7.2 140.3 %all-gather.5.cloned.1.call-start = ((), (), s32[]{:S(2)}) async-start(), calls=%async_computation.4 | async-start | bytes 2621440 | tf_op jit(solution)/shard_map/all_gather | solution.py:268
  9.7 9.3 %collective-permute-start = (bf16[256,512]{0,1:T(8,128)(2,1)S(1)}, bf16[256,512]{0,1:T(8,128)(2,1)S(1)}, u32[]{:S(2)}, u32[]{:S(2)}) collective-permute-start(bf16[256,512]{0,1:T(8,128)(2,1)S(1)} %pad_maximum_fusion.11), channel_id=1, source_target_pairs={{0,4},{4,0},{1,5},{5,1},{2,6},{6,2},{3,7},{7,3},{8,12},{12,8},{9,1... | collective-permute-start | bytes 786440 | tf_op jit(solution)/shard_map/ppermute | solution.py:245
  19.9 183.5 %all-gather.7.cloned.1.call-start = ((), (), s32[]{:S(2)}) async-start(), calls=%async_computation.5 | async-start | bytes 2621440 | tf_op jit(solution)/shard_map/all_gather | solution.py:268
  64.1 8.6 %collective-permute-start.1 = (bf16[256,512]{0,1:T(8,128)(2,1)S(1)}, bf16[256,512]{0,1:T(8,128)(2,1)S(1)}, u32[]{:S(2)}, u32[]{:S(2)}) collective-permute-start(bf16[256,512]{0,1:T(8,128)(2,1)S(1)} %pad_maximum_fusion.12), channel_id=1, source_target_pairs={{0,4},{4,0},{1,5},{5,1},{2,6},{6,2},{3,7},{7,3},{8,12},{12,8},{9,1... | collective-permute-start | bytes 786440 | tf_op jit(solution)/shard_map/ppermute | solution.py:245
  73.7 230.8 %all-gather.9.cloned.1.call-start = ((), (), s32[]{:S(2)}) async-start(), calls=%async_computation.6 | async-start | bytes 7864320 | tf_op jit(solution)/shard_map/all_gather | solution.py:268
  74.0 19.1 %collective-permute-start.2 = (bf16[256,1536]{1,0:T(8,128)(2,1)S(1)}, bf16[256,1536]{1,0:T(8,128)(2,1)S(1)}, u32[]{:S(2)}, u32[]{:S(2)}) collective-permute-start(bf16[256,1536]{1,0:T(8,128)(2,1)S(1)} %pad_maximum_fusion.10), channel_id=1, source_target_pairs={{0,4},{4,0},{1,5},{5,1},{2,6},{6,2},{3,7},{7,3},{8,12},{12,8},{9,1... | collective-permute-start | bytes 2359304 | tf_op jit(solution)/shard_map/ppermute | solution.py:245
  94.9 228.9 %all-gather.11.cloned.1.call-start = ((), (), s32[]{:S(2)}) async-start(), calls=%async_computation.7 | async-start | bytes 3932160 | tf_op jit(solution)/shard_map/all_gather | solution.py:268
  96.2 49.6 %collective-permute-start.3 = (bf16[256,768]{0,1:T(8,128)(2,1)S(1)}, bf16[256,768]{0,1:T(8,128)(2,1)S(1)}, u32[]{:S(2)}, u32[]{:S(2)}) collective-permute-start(bf16[256,768]{0,1:T(8,128)(2,1)S(1)} %get-tuple-element.145), channel_id=1, source_target_pairs={{0,4},{4,0},{1,5},{5,1},{2,6},{6,2},{3,7},{7,3},{8,12},{12,8},{9,1... | collective-permute-start | bytes 1179656 | tf_op jit(solution)/shard_map/ppermute | solution.py:245
  97.0 69.2 %copy-start.64 = (f32[128]{0:T(128)}, f32[128]{0:T(128)S(1)}, u32[]{:S(2)}) copy-start(f32[128]{0:T(128)S(1)} %convert_element_type.188) | copy-start | bytes 1540
  102.0 68.4 %copy-start.59 = (f32[128]{0:T(128)}, f32[128]{0:T(128)S(1)}, u32[]{:S(2)}) copy-start(f32[128]{0:T(128)S(1)} %convert_element_type.186) | copy-start | bytes 1540
  146.9 580.4 %reduce-scatter.7.cloned.1.call-start = ((), (), s32[]{:S(2)}) async-start(), calls=%async_computation.9 | async-start | bytes 2621440 | tf_op jit(solution)/shard_map/reduce_scatter | solution.py:272
  412.3 44.4 %copy-start.18 = (bf16[1,256,2048]{2,1,0:T(8,128)(2,1)S(1)}, bf16[1,256,2048]{2,1,0:T(8,128)(2,1)}, u32[]{:S(2)}) copy-start(bf16[1,256,2048]{2,1,0:T(8,128)(2,1)} %param.19) | copy-start | bytes 3145732
  544.0 186.9 %reduce-scatter.5.cloned.1.call-start = ((), (), s32[]{:S(2)}) async-start(), calls=%async_computation.8 | async-start | bytes 2621440 | tf_op jit(solution)/shard_map/reduce_scatter | solution.py:272
  584.7 157.7 %reduce-scatter.11.cloned.1.call-start = ((), (), s32[]{:S(2)}) async-start(), calls=%async_computation.11 | async-start | bytes 3932160 | tf_op jit(solution)/shard_map/reduce_scatter | solution.py:272
  596.2 212.9 %reduce-scatter.9.cloned.1.call-start = ((), (), s32[]{:S(2)}) async-start(), calls=%async_computation.10 | async-start | bytes 7864320 | tf_op jit(solution)/shard_map/reduce_scatter | solution.py:272
  636.9 42.5 %copy-start.3 = (bf16[1,256,2048]{2,1,0:T(8,128)(2,1)S(1)}, bf16[1,256,2048]{2,1,0:T(8,128)(2,1)}, u32[]{:S(2)}) copy-start(bf16[1,256,2048]{2,1,0:T(8,128)(2,1)} %param.18) | copy-start | bytes 3145732
  636.9 42.5 %copy-start.52 = (f32[2048]{0:T(1024)S(1)}, f32[2048]{0:T(1024)}, u32[]{:S(2)}) copy-start(f32[2048]{0:T(1024)} %copy-done.51) | copy-start | bytes 24580
  636.9 42.5 %copy-start.58 = (f32[256]{0:T(256)S(1)}, f32[256]{0:T(256)}, u32[]{:S(2)}) copy-start(f32[256]{0:T(256)} %copy-done.57) | copy-start | bytes 3076
  679.4 44.6 %copy-start.4 = (f32[256,2048]{1,0:T(8,128)S(1)}, f32[256,2048]{1,0:T(8,128)}, u32[]{:S(2)}) copy-start(f32[256,2048]{1,0:T(8,128)} %scatter_tokens.7) | copy-start | bytes 6291460
  679.4 44.6 %copy-start.61 = (f32[256]{0:T(256)S(1)}, f32[256]{0:T(256)}, u32[]{:S(2)}) copy-start(f32[256]{0:T(256)} %get-tuple-element.174) | copy-start | bytes 3076
  728.2 9.9 %collective-permute-start.5 = (bf16[256,512]{1,0:T(8,128)(2,1)S(1)}, bf16[256,512]{1,0:T(8,128)(2,1)S(1)}, u32[]{:S(2)}, u32[]{:S(2)}) collective-permute-start(bf16[256,512]{1,0:T(8,128)(2,1)S(1)} %constant_dynamic-slice_fusion.5), channel_id=1, source_target_pairs={{0,4},{4,0},{1,5},{5,1},{2,6},{6,2},{3,7},{7,3},{8,12},{12,8},{9,1... | collective-permute-start | bytes 786440 | tf_op jit(solution)/shard_map/ppermute | solution.py:245
  731.9 10.5 %collective-permute-start.4 = (bf16[256,512]{1,0:T(8,128)(2,1)S(1)}, bf16[256,512]{1,0:T(8,128)(2,1)S(1)}, u32[]{:S(2)}, u32[]{:S(2)}) collective-permute-start(bf16[256,512]{1,0:T(8,128)(2,1)S(1)} %constant_dynamic-slice_fusion.7), channel_id=1, source_target_pairs={{0,4},{4,0},{1,5},{5,1},{2,6},{6,2},{3,7},{7,3},{8,12},{12,8},{9,1... | collective-permute-start | bytes 786440 | tf_op jit(solution)/shard_map/ppermute | solution.py:245
  743.6 73.3 %collective-permute-start.7 = (bf16[256,768]{1,0:T(8,128)(2,1)S(1)}, bf16[256,768]{1,0:T(8,128)(2,1)S(1)}, u32[]{:S(2)}, u32[]{:S(2)}) collective-permute-start(bf16[256,768]{1,0:T(8,128)(2,1)S(1)} %get-tuple-element.141), channel_id=1, source_target_pairs={{0,4},{4,0},{1,5},{5,1},{2,6},{6,2},{3,7},{7,3},{8,12},{12,8},{9,1... | collective-permute-start | bytes 1179656 | tf_op jit(solution)/shard_map/ppermute | solution.py:245
  811.1 19.7 %collective-permute-start.6 = (bf16[256,1536]{1,0:T(8,128)(2,1)}, bf16[256,1536]{1,0:T(8,128)(2,1)}, u32[]{:S(2)}, u32[]{:S(2)}) collective-permute-start(bf16[256,1536]{1,0:T(8,128)(2,1)} %constant_dynamic-slice_fusion.4), channel_id=1, source_target_pairs={{0,4},{4,0},{1,5},{5,1},{2,6},{6,2},{3,7},{7,3},{8,12},{12,8},{9,1... | collective-permute-start | bytes 2359304 | tf_op jit(solution)/shard_map/ppermute | solution.py:245
  (73 other events, 497.6 us)
Sparse Core Ops, SparseCore 0:
  20.1 47.3 all-gather.4
  73.8 46.2 all-gather.6
  122.2 114.0 all-gather.8
  237.8 61.6 all-gather.10
  544.1 44.2 reduce-scatter.6
  590.6 43.1 reduce-scatter.4
  636.0 59.5 reduce-scatter.10
  698.0 111.0 reduce-scatter.8
